TPU v7x, 32 devices: a whole 2x2x4 slice. The times are simulated.
32 devices in a mesh: expert: 8 (over y, x, core), tensor: 4 (over z).
Axes of the slice: x: 2, y: 2, z: 4, core: 2. Of those that a mesh axis runs over, the one named last changes fastest.
Arguments:
- tokens: bfloat16 [512, 4096], P(('expert', 'tensor')), may hold values from -6 to 6
- grad_out: bfloat16 [512, 4096], P(('expert', 'tensor')), may hold values from -1.5 to 1.5
- routes: int32 [512, 8], P(('expert', 'tensor')), may hold values from 0 to 15, all different within a row; in each aligned block of 16 rows (0 to 15, 16 to 31, ...) at most 12 rows name the same one
- gate_probs: bfloat16 [512, 8], P(('expert', 'tensor')), may hold values from 0.019897461 to 0.29882812
- w_gate: bfloat16 [16, 1536, 4096], P('expert', 'tensor'), may hold values from -0.09375 to 0.09375
- w_up: bfloat16 [16, 1536, 4096], P('expert', 'tensor'), may hold values from -0.09375 to 0.09375
- w_down: bfloat16 [16, 1536, 4096], P('expert', 'tensor'), may hold values from -0.15625 to 0.15625
Outputs:
- d_tokens: bfloat16 [512, 4096], P(('expert', 'tensor'))
- d_probs: bfloat16 [512, 8], P(('expert', 'tensor'))
- d_gate: bfloat16 [16, 1536, 4096], P('expert', 'tensor')
- d_up: bfloat16 [16, 1536, 4096], P('expert', 'tensor')
- d_down: bfloat16 [16, 1536, 4096], P('expert', 'tensor')
Inputs may be any that keep to these rules, and one draw needn't show every extreme that they name: `routes`: each token names 8 different experts. In each aligned block of 16 tokens (the tokens of one device) no expert is named by more than 12 tokens, a bound that some block reaches.
All inputs are finite; a program needn't handle non-finite values.
Results may differ from a plain program's by a relative error of at most 0.019.
Values may be sent and summed in bfloat16 or wider, within the bound.
A program may use at most 256 MiB of HBM per device.

v0:
```python
import jax
import jax.numpy as jnp
from jax import lax
from jax.sharding import PartitionSpec as P


def slot_layout(routes, experts_all, capacity):
    flat_routes = routes.reshape(-1)
    expert_ids = jnp.arange(experts_all, dtype=jnp.int32)
    onehot = (flat_routes[:, None] == expert_ids[None, :]).astype(jnp.int32)
    slot_rank = jnp.sum(onehot * (jnp.cumsum(onehot, axis=0) - 1), axis=1)
    slot_index = flat_routes * capacity + slot_rank
    slot_ids = jnp.arange(experts_all * capacity, dtype=jnp.int32)
    return (slot_index[None, :] == slot_ids[:, None]).astype(jnp.bfloat16)


def per_device(tokens, grad_out, routes, gate_probs, w_gate, w_up, w_down):
    tok_count = tokens.shape[0]
    top_count = routes.shape[1]
    width = tokens.shape[1]
    owners = lax.axis_size("expert")
    tensor_size = lax.axis_size("tensor")
    local_experts = w_gate.shape[0]
    experts_all = local_experts * owners
    capacity = max(2, 3 * tok_count * top_count // (2 * experts_all))
    slot_total = experts_all * capacity
    per_owner = local_experts * capacity
    sources = owners * tensor_size
    assign = slot_layout(routes, experts_all, capacity)
    assign_tok = jnp.sum(assign.reshape(slot_total, tok_count, top_count), axis=2)
    send_x = jnp.dot(assign_tok, tokens, preferred_element_type=jnp.float32).astype(jnp.bfloat16)
    send_dy = jnp.dot(assign_tok, grad_out, preferred_element_type=jnp.float32).astype(jnp.bfloat16)
    send_prob = jnp.dot(assign, gate_probs.reshape(-1), preferred_element_type=jnp.float32).astype(
        jnp.bfloat16
    )
    send_x = send_x.reshape(owners, 1, per_owner, width)
    send_dy = send_dy.reshape(owners, 1, per_owner, width)
    send_prob = send_prob.reshape(owners, 1, per_owner)
    moved = (
        lax.all_to_all(send_x, "expert", split_axis=0, concat_axis=0, tiled=True),
        lax.all_to_all(send_dy, "expert", split_axis=0, concat_axis=0, tiled=True),
        lax.all_to_all(send_prob, "expert", split_axis=0, concat_axis=0, tiled=True),
    )
    received = (
        lax.all_gather(moved[0], "tensor", axis=1, tiled=True),
        lax.all_gather(moved[1], "tensor", axis=1, tiled=True),
        lax.all_gather(moved[2], "tensor", axis=1, tiled=True),
    )
    rows_x = received[0].reshape(sources, local_experts, capacity, width)
    rows_dy = received[1].reshape(sources, local_experts, capacity, width)
    rows_prob = received[2].reshape(sources, local_experts, capacity).astype(jnp.float32)[..., None]
    gate = jnp.einsum("sjcd,jfd->sjcf", rows_x, w_gate, preferred_element_type=jnp.float32)
    up_val = jnp.einsum("sjcd,jfd->sjcf", rows_x, w_up, preferred_element_type=jnp.float32)
    sigma = jax.nn.sigmoid(gate)
    hidden = gate * sigma * up_val
    back = jnp.einsum("sjcd,jfd->sjcf", rows_dy, w_down, preferred_element_type=jnp.float32)
    dprob_part = jnp.sum(hidden * back, axis=3)
    scaled = (rows_prob * rows_dy).astype(jnp.bfloat16)
    d_down = jnp.einsum(
        "sjcf,sjcd->jfd", hidden.astype(jnp.bfloat16), scaled, preferred_element_type=jnp.float32
    ).astype(jnp.bfloat16)
    d_hidden = rows_prob * back
    d_gate_pre = (d_hidden * up_val * sigma * (1.0 + gate * (1.0 - sigma))).astype(jnp.bfloat16)
    d_up_pre = (d_hidden * gate * sigma).astype(jnp.bfloat16)
    d_gate = jnp.einsum(
        "sjcf,sjcd->jfd", d_gate_pre, rows_x, preferred_element_type=jnp.float32
    ).astype(jnp.bfloat16)
    d_up = jnp.einsum(
        "sjcf,sjcd->jfd", d_up_pre, rows_x, preferred_element_type=jnp.float32
    ).astype(jnp.bfloat16)
    partial_value = jnp.einsum(
        "sjcf,jfd->sjcd", d_gate_pre, w_gate, preferred_element_type=jnp.float32
    )
    partial_value = partial_value + jnp.einsum(
        "sjcf,jfd->sjcd", d_up_pre, w_up, preferred_element_type=jnp.float32
    )
    block_terms = partial_value.astype(jnp.bfloat16).reshape(sources, per_owner, width)
    block_probs = dprob_part.astype(jnp.bfloat16).reshape(sources, per_owner)
    arrived = (
        lax.all_to_all(block_terms, ("expert", "tensor"), split_axis=0, concat_axis=0, tiled=True),
        lax.all_to_all(block_probs, ("expert", "tensor"), split_axis=0, concat_axis=0, tiled=True),
    )
    slot_grad = jnp.sum(
        arrived[0].reshape(owners, tensor_size, per_owner, width), axis=1, dtype=jnp.float32
    ).astype(jnp.bfloat16)
    slot_dprob = jnp.sum(
        arrived[1].reshape(owners, tensor_size, per_owner), axis=1, dtype=jnp.float32
    ).astype(jnp.bfloat16)
    slot_grad = slot_grad.reshape(slot_total, width)
    slot_dprob = slot_dprob.reshape(slot_total)
    d_tokens = jnp.dot(assign_tok.T, slot_grad, preferred_element_type=jnp.float32).astype(
        jnp.bfloat16
    )
    d_probs = jnp.dot(assign.T, slot_dprob, preferred_element_type=jnp.float32)
    d_probs = d_probs.reshape(tok_count, top_count).astype(jnp.bfloat16)
    return (d_tokens, d_probs, d_gate, d_up, d_down)


def solution(mesh):
    in_specs = (
        P(("expert", "tensor"), None),
        P(("expert", "tensor"), None),
        P(("expert", "tensor"), None),
        P(("expert", "tensor"), None),
        P("expert", "tensor", None),
        P("expert", "tensor", None),
        P("expert", "tensor", None),
    )
    out_specs = (
        P(("expert", "tensor"), None),
        P(("expert", "tensor"), None),
        P("expert", "tensor", None),
        P("expert", "tensor", None),
        P("expert", "tensor", None),
    )
    return jax.shard_map(
        per_device, mesh=mesh, in_specs=in_specs, out_specs=out_specs, check_vma=False
    )
```

profile of v0, /device:TPU:0, one launch (start us, length us, event | category | flops | bytes accessed | tf_op | source)
XLA Modules:
  0.0 475.2 jit_solution(4111333621195504892)
XLA Ops:
  9.4 26.1 %all_to_all.26 = bf16[8,1,24,4096]{3,2,1,0:T(8,128)(2,1)} all-to-all(bf16[8,1,24,4096]{3,2,1,0:T(8,128)(2,1)S(1)} %bitcast.94), channel_id=1, replica_groups=mesh['expert'=8,'tensor'=4] {'expert'}, dimensions={0} | all-to-all | bytes 3145728 | tf_op jit(solution)/shard_map/all_to_all | solution.py:40
  36.2 24.1 %all_to_all.27 = bf16[8,1,24,4096]{3,2,1,0:T(8,128)(2,1)} all-to-all(bf16[8,1,24,4096]{3,2,1,0:T(8,128)(2,1)S(1)} %bitcast.95), channel_id=1, replica_groups=mesh['expert'=8,'tensor'=4] {'expert'}, dimensions={0} | all-to-all | bytes 3145728 | tf_op jit(solution)/shard_map/all_to_all | solution.py:41
  60.8 7.0 %all_to_all.28 = bf16[8,1,24]{2,1,0:T(2,128)(2,1)S(1)} all-to-all(bf16[8,1,24]{2,1,0:T(2,128)(2,1)S(1)} %reshape.134), channel_id=1, replica_groups=mesh['expert'=8,'tensor'=4] {'expert'}, dimensions={0} | all-to-all | bytes 768 | tf_op jit(solution)/shard_map/all_to_all | solution.py:42
  67.8 15.9 %all_gather.9 = bf16[8,4,24]{2,0,1:T(8,128)(2,1)S(1)} all-gather(bf16[8,1,24]{2,0,1:T(8,128)(2,1)S(1)} %copy.73), channel_id=1, replica_groups=mesh['expert'=8,'tensor'=4] {'tensor'}, dimensions={1}, use_global_device_ids=true | all-gather | bytes 1920 | tf_op jit(solution)/shard_map/all_gather | solution.py:47
  83.9 66.6 %all-gather.5.cloned.1.call-done = bf16[8,4,24,4096]{3,2,0,1:T(8,128)(2,1)} async-done(((bf16[8,1,24,4096]{3,2,0,1:T(8,128)(2,1)}), bf16[8,4,24,4096]{3,2,0,1:T(8,128)(2,1)}) %all-gather.5.cloned.1.call-update) | async-done | bytes 6291472 | tf_op jit(solution)/shard_map/all_gather | solution.py:45
  150.5 10.4 %copy.81 = bf16[8,4,24,4096]{3,1,0,2:T(4,128)(2,1)} copy(bf16[8,4,24,4096]{3,2,0,1:T(8,128)(2,1)} %all-gather.5.cloned.1.call-done) | data formatting | bytes 12582912 | tf_op jit(solution)/shard_map/all_gather | solution.py:45
  160.9 10.0 %reshape.116 = bf16[32,2,12,4096]{3,0,2,1:T(8,128)(2,1)} reshape(bf16[8,4,24,4096]{3,1,0,2:T(4,128)(2,1)} %copy.81) | data formatting | bytes 12582912 | tf_op jit(solution)/shard_map/reshape | solution.py:49
  170.9 9.3 %fusion.10 = f32[32,2,12,384]{3,0,2,1:T(8,128)} fusion(bf16[32,2,12,4096]{3,0,2,1:T(8,128)(2,1)} %reshape.116, bf16[2,384,4096]{2,1,0:T(8,128)(2,1)} %param.12), kind=kOutput, calls=%fused_computation.19 | convolution fusion | flops 2415919104 | bytes 13762560 | tf_op jit(solution)/shard_map/sjcd,jfd->sjcf/dot_general | solution.py:53
  180.2 4.4 fusion.16
  184.6 81.1 %all-gather.3.cloned.1.call-done = bf16[8,4,24,4096]{3,2,0,1:T(8,128)(2,1)} async-done(((bf16[8,1,24,4096]{3,2,0,1:T(8,128)(2,1)}), bf16[8,4,24,4096]{3,2,0,1:T(8,128)(2,1)}) %all-gather.3.cloned.1.call-update) | async-done | bytes 6291472 | tf_op jit(solution)/shard_map/all_gather | solution.py:46
  265.7 10.3 %copy.78 = bf16[8,4,24,4096]{3,1,0,2:T(4,128)(2,1)} copy(bf16[8,4,24,4096]{3,2,0,1:T(8,128)(2,1)} %all-gather.3.cloned.1.call-done) | data formatting | bytes 12582912 | tf_op jit(solution)/shard_map/all_gather | solution.py:46
  276.1 10.0 %reshape.114 = bf16[32,2,12,4096]{3,0,2,1:T(8,128)(2,1)} reshape(bf16[8,4,24,4096]{3,1,0,2:T(4,128)(2,1)} %copy.78) | data formatting | bytes 12582912 | tf_op jit(solution)/shard_map/reshape | solution.py:50
  286.1 9.3 %multiply_reduce_fusion = (bf16[32,2,12]{0,2,1:T(8,128)(2,1)S(1)}, bf16[32,2,12,384]{3,0,2,1:T(8,128)(2,1)S(1)}, bf16[32,2,12,384]{3,0,2,1:T(8,128)(2,1)S(1)}) fusion(f32[32,2,12,384]{3,0,2,1:T(8,128)} %fusion.10, f32[32,2,12,384]{3,0,2,1:T(8,128)} %fusion.16, f32[32,2,12]{0,2,1:T(8,128)S(1)} %copy.75, bf16[32,2,12,4096]{3,0,2,1:T(8,128)(2,1)} %reshape.114, ...), kind=kOutput, calls=%fused_computation.22 | convolution fusion | flops 2421226752 | bytes 16126464 | tf_op jit(solution)/shard_map/sjcd,jfd->sjcf/dot_general | solution.py:56
  295.4 6.3 %fusion = f32[2,32,12,4096]{3,1,2,0:T(8,128)} fusion(bf16[32,2,12,384]{3,0,2,1:T(8,128)(2,1)S(1)} %get-tuple-element.6, bf16[2,384,4096]{2,1,0:T(8,128)(2,1)S(1)} %bitcast.99), kind=kOutput, calls=%fused_computation.5 | convolution fusion | flops 2415919104 | bytes 19464192 | tf_op jit(solution)/shard_map/sjcf,jfd->sjcd/dot_general | solution.py:71
  302.5 2.8 all-to-all-start.4
  305.3 8.4 %add_convert_fusion = bf16[2,32,12,4096]{3,1,2,0:T(8,128)(2,1)S(1)} fusion(f32[2,32,12,4096]{3,1,2,0:T(8,128)} %fusion, bf16[32,2,12,384]{3,0,2,1:T(8,128)(2,1)S(1)} %get-tuple-element.7, bf16[2,384,4096]{2,1,0:T(8,128)(2,1)} %param.12), kind=kOutput, calls=%fused_computation.4 | convolution fusion | flops 2422210560 | bytes 25755648 | tf_op jit(solution)/shard_map/sjcf,jfd->sjcd/dot_general | solution.py:74
  313.7 6.1 %copy.82 = bf16[32,24,4096]{2,1,0:T(8,128)(2,1)} copy(bf16[32,24,4096]{2,0,1:T(8,128)(2,1)S(1)} %bitcast.87) | data formatting | bytes 12582912 | tf_op jit(solution)/shard_map/reshape | solution.py:77
  319.8 6.2 %all-to-all-start.3 = ((bf16[32,24,4096]{2,1,0:T(8,128)(2,1)}), bf16[32,24,4096]{2,1,0:T(8,128)(2,1)}, u32[]{:S(2)}, u32[]{:S(2)}) async-start(bf16[32,24,4096]{2,1,0:T(8,128)(2,1)} %copy.82), calls=%async_computation.3 | async-start | bytes 12582912 | tf_op jit(solution)/shard_map/all_to_all | solution.py:80
  326.0 9.1 %bitcast_convert_fusion.1 = bf16[2,384,4096]{2,1,0:T(8,128)(2,1)} fusion(bf16[32,2,12,384]{3,0,2,1:T(8,128)(2,1)S(1)} %get-tuple-element.7, bf16[32,2,12,4096]{3,0,2,1:T(8,128)(2,1)} %reshape.116), kind=kOutput, calls=%fused_computation.1 | convolution fusion | flops 2419064832 | bytes 13172736 | tf_op jit(solution)/shard_map/sjcf,sjcd->jfd/dot_general | solution.py:68
  335.1 5.4 %bitcast_convert_fusion.2 = bf16[2,384,4096]{2,1,0:T(8,128)(2,1)} fusion(bf16[32,2,12,384]{3,0,2,1:T(8,128)(2,1)S(1)} %get-tuple-element.6, bf16[32,2,12,4096]{3,0,2,1:T(8,128)(2,1)S(1)} %bitcast.89), kind=kOutput, calls=%fused_computation.2 | convolution fusion | flops 2419064832 | bytes 13172736 | tf_op jit(solution)/shard_map/sjcf,sjcd->jfd/dot_general | solution.py:65
  340.5 5.8 %bitcast_convert_fusion = bf16[2,384,4096]{2,1,0:T(8,128)(2,1)} fusion(bf16[32,2,12,4096]{3,0,2,1:T(8,128)(2,1)S(1)} %bitcast.91, f32[32,2,12]{0,2,1:T(8,128)S(1)} %copy.75, f32[32,2,12,384]{3,0,2,1:T(8,128)S(1)} %copy-done.5, f32[32,2,12,384]{3,0,2,1:T(8,128)S(1)} %copy-done.6), kind=kOutput, calls=%fused_computation | convolution fusion | flops 2430271488 | bytes 14945280 | tf_op jit(solution)/shard_map/sjcf,sjcd->jfd/dot_general | solution.py:59
  347.4 115.5 %all-to-all-done.3 = bf16[32,24,4096]{2,1,0:T(8,128)(2,1)} async-done(((bf16[32,24,4096]{2,1,0:T(8,128)(2,1)}), bf16[32,24,4096]{2,1,0:T(8,128)(2,1)}, u32[]{:S(2)}, u32[]{:S(2)}) %all-to-all-start.3) | async-done | bytes 6291488 | tf_op jit(solution)/shard_map/all_to_all | solution.py:80
  462.9 4.1 bitcast_reduce_fusion
  466.9 1.0 convolution_convert_fusion.2
  (66 shorter events, 5.4 us)
Async XLA Ops:
  7.2 1.7 copy-start
  7.2 28.4 %copy-start.3 = (bf16[16,4096]{1,0:T(8,128)(2,1)S(1)}, bf16[16,4096]{1,0:T(8,128)(2,1)}, u32[]{:S(2)}) copy-start(bf16[16,4096]{1,0:T(8,128)(2,1)} %param.8) | copy-start | bytes 393220
  7.2 143.3 %all-gather.5.cloned.1.call-start = ((), (), s32[]{:S(2)}) async-start(), calls=%async_computation.6 | async-start | bytes 7864320 | tf_op jit(solution)/shard_map/all_gather | solution.py:45
  8.8 51.5 %copy-start.4 = (bf16[16,8]{0,1:T(8,128)(2,1)S(1)}, bf16[16,8]{0,1:T(8,128)(2,1)}, u32[]{:S(2)}) copy-start(bf16[16,8]{0,1:T(8,128)(2,1)} %param.10) | copy-start | bytes 772
  35.5 230.2 %all-gather.3.cloned.1.call-start = ((), (), s32[]{:S(2)}) async-start(), calls=%async_computation.5 | async-start | bytes 7864320 | tf_op jit(solution)/shard_map/all_gather | solution.py:46
  160.9 19.3 %slice-start.4 = ((s8[6291456]{0:T(1024)(128)(4,1)}), s8[2097152]{0:T(1024)(128)(4,1)S(1)}, s32[]{:S(2)}) async-start(s8[6291456]{0:T(1024)(128)(4,1)} %bitcast.96), calls=%async_computation.11 | async-start | bytes 4194304
  170.9 9.3 %copy-start.2 = (bf16[32,2,12,4096]{3,0,2,1:T(8,128)(2,1)S(1)}, bf16[32,2,12,4096]{3,0,2,1:T(8,128)(2,1)}, u32[]{:S(2)}) copy-start(bf16[32,2,12,4096]{3,0,2,1:T(8,128)(2,1)} %reshape.116) | copy-start | bytes 18874372
  170.9 9.3 %slice-start.5 = ((s8[6291456]{0:T(1024)(128)(4,1)}), s8[4194304]{0:T(1024)(128)(4,1)S(1)}, s32[]{:S(2)}) async-start(s8[6291456]{0:T(1024)(128)(4,1)} %bitcast.96), calls=%async_computation.12 | async-start | bytes 8388608
  276.0 19.3 %slice-start.6 = ((s8[6291456]{0:T(1024)(128)(4,1)}), s8[2097152]{0:T(1024)(128)(4,1)S(1)}, s32[]{:S(2)}) async-start(s8[6291456]{0:T(1024)(128)(4,1)} %bitcast.98), calls=%async_computation.13 | async-start | bytes 4194304
  286.1 9.3 %slice-start.7 = ((s8[6291456]{0:T(1024)(128)(4,1)}), s8[4194304]{0:T(1024)(128)(4,1)S(1)}, s32[]{:S(2)}) async-start(s8[6291456]{0:T(1024)(128)(4,1)} %bitcast.98), calls=%async_computation.14 | async-start | bytes 8388608
  302.5 17.3 %all-to-all-start.4 = ((bf16[32,1,24]{2,1,0:T(2,128)(2,1)}), bf16[32,1,24]{2,1,0:T(2,128)(2,1)S(1)}, u32[]{:S(2)}, u32[]{:S(2)}) async-start(bf16[32,1,24]{2,1,0:T(2,128)(2,1)} %copy.85), calls=%async_computation.4 | async-start | bytes 32768 | tf_op jit(solution)/shard_map/all_to_all | solution.py:81
  319.8 15.3 %slice-start = ((s8[6291456]{0:T(1024)(128)(4,1)}), s8[2097152]{0:T(1024)(128)(4,1)S(1)}, s32[]{:S(2)}) async-start(s8[6291456]{0:T(1024)(128)(4,1)} %bitcast.88), calls=%async_computation.7 | async-start | bytes 4194304
  319.8 143.1 %all-to-all-start.3 = ((bf16[32,24,4096]{2,1,0:T(8,128)(2,1)}), bf16[32,24,4096]{2,1,0:T(8,128)(2,1)}, u32[]{:S(2)}, u32[]{:S(2)}) async-start(bf16[32,24,4096]{2,1,0:T(8,128)(2,1)} %copy.82), calls=%async_computation.3 | async-start | bytes 12582912 | tf_op jit(solution)/shard_map/all_to_all | solution.py:80
  326.0 9.1 %slice-start.1 = ((s8[6291456]{0:T(1024)(128)(4,1)}), s8[4194304]{0:T(1024)(128)(4,1)S(1)}, s32[]{:S(2)}) async-start(s8[6291456]{0:T(1024)(128)(4,1)} %bitcast.88), calls=%async_computation.8 | async-start | bytes 8388608
  326.0 14.5 %slice-start.2 = ((s8[6291456]{0:T(1024)(128)(4,1)}), s8[4194304]{0:T(1024)(128)(4,1)S(1)}, s32[]{:S(2)}) async-start(s8[6291456]{0:T(1024)(128)(4,1)} %bitcast.90), calls=%async_computation.9 | async-start | bytes 8388608
  335.1 5.4 %slice-start.3 = ((s8[6291456]{0:T(1024)(128)(4,1)}), s8[2097152]{0:T(1024)(128)(4,1)S(1)}, s32[]{:S(2)}) async-start(s8[6291456]{0:T(1024)(128)(4,1)} %bitcast.90), calls=%async_computation.10 | async-start | bytes 4194304
  335.1 5.4 %copy-start.5 = (f32[32,2,12,384]{3,0,2,1:T(8,128)S(1)}, f32[32,2,12,384]{3,0,2,1:T(8,128)}, u32[]{:S(2)}) copy-start(f32[32,2,12,384]{3,0,2,1:T(8,128)} %fusion.10) | copy-start | bytes 3538948
  335.1 5.4 %copy-start.6 = (f32[32,2,12,384]{3,0,2,1:T(8,128)S(1)}, f32[32,2,12,384]{3,0,2,1:T(8,128)}, u32[]{:S(2)}) copy-start(f32[32,2,12,384]{3,0,2,1:T(8,128)} %fusion.16) | copy-start | bytes 3538948
  340.5 127.4 %copy-start.1 = (bf16[16,4096]{1,0:T(8,128)(2,1)S(1)}, bf16[16,4096]{1,0:T(8,128)(2,1)}, u32[]{:S(2)}) copy-start(bf16[16,4096]{1,0:T(8,128)(2,1)} %param.7) | copy-start | bytes 393220
Sparse Core Ops, SparseCore 0:
  35.6 114.8 all-gather.4
  152.1 113.5 all-gather.2
where the time goes:
time: 484 us; the launch traced here: 475 us
  waiting for transfers between devices  263 us (54%)
  blocking collectives  73.1 us (15%)
  matrix products  60.5 us (12%)
  local copies, waits for them, and re-layouts  49.9 us (10%)
  between operations  14.8 us (3%)
  starting transfers between devices  9.1 us (2%)
    all_to_all x1, waiting for transfers between devices, per_device(): lax.all_to_all(block_terms, ('expert', 'tensor'), split_axis=0, concat_ax...  115 us
    all_gather x1, waiting for transfers between devices, per_device(): lax.all_gather(moved[1], 'tensor', axis=1, tiled=True)  81.1 us
    all_gather x1, waiting for transfers between devices, per_device(): lax.all_gather(moved[0], 'tensor', axis=1, tiled=True)  66.6 us
    all_to_all x1, blocking collectives, per_device(): lax.all_to_all(send_x, 'expert', split_axis=0, concat_axis=0, tiled=True)  26.1 us
    all_to_all x1, blocking collectives, per_device(): lax.all_to_all(send_dy, 'expert', split_axis=0, concat_axis=0, tiled=True)  24.1 us
    all_gather x1, blocking collectives, per_device(): lax.all_gather(moved[2], 'tensor', axis=1, tiled=True)  15.9 us
    all_gather x1, local copies, waits for them, and re-layouts, per_device(): lax.all_gather(moved[0], 'tensor', axis=1, tiled=True)  10.4 us
    all_gather x1, local copies, waits for them, and re-layouts, per_device(): lax.all_gather(moved[1], 'tensor', axis=1, tiled=True)  10.3 us
  transfers between devices with their start and end apart: 4, of which 3 were waited for; matrix products, arithmetic and copies ran while one was open for 15% of the time, Pallas kernels for 0%

commit v1 on v0

v1 whole, which is shorter than its diff:
```python
import jax
import jax.numpy as jnp
from jax import lax
from jax.sharding import PartitionSpec as P

AXES = ("expert", "tensor")


def per_device(tokens, grad_out, routes, gate_probs, w_gate, w_up, w_down):
    local, units, width = w_gate.shape
    first = lax.axis_index("expert") * local
    mine = first + jnp.arange(local, dtype=jnp.int32)
    owners = lax.axis_size("expert")
    ids = jnp.arange(local * owners, dtype=jnp.int32)
    hit = routes[:, :, None] == ids[None, None, :]
    table = jnp.sum(jnp.where(hit, gate_probs[:, :, None].astype(jnp.float32), 0.0), axis=1)
    table = table.astype(jnp.bfloat16)
    rows_x = lax.all_gather(tokens, AXES, axis=0, tiled=True)
    rows_g = lax.all_gather(grad_out, AXES, axis=0, tiled=True)
    probs = lax.all_gather(table, AXES, axis=0, tiled=True)
    probs = lax.dynamic_slice_in_dim(probs, first, local, axis=1).astype(jnp.float32)
    count = rows_x.shape[0]
    wg = w_gate.reshape(local * units, width)
    wu = w_up.reshape(local * units, width)
    wd = w_down.reshape(local * units, width)
    nt = (((1,), (1,)), ((), ()))
    tn = (((0,), (0,)), ((), ()))
    f32 = jnp.float32
    gate = lax.dot_general(rows_x, wg, nt, preferred_element_type=f32)
    up = lax.dot_general(rows_x, wu, nt, preferred_element_type=f32)
    back = lax.dot_general(rows_g, wd, nt, preferred_element_type=f32)
    sigma = jax.nn.sigmoid(gate)
    act = gate * sigma
    hidden = act * up
    p = jnp.broadcast_to(probs[:, :, None], (count, local, units)).reshape(count, local * units)
    d_hidden = p * back
    dgp = (d_hidden * up * sigma * (1.0 + gate * (1.0 - sigma))).astype(jnp.bfloat16)
    dup = (d_hidden * act).astype(jnp.bfloat16)
    hs = (hidden * p).astype(jnp.bfloat16)
    dprob = jnp.sum((hidden * back).reshape(count, local, units), axis=2)
    part = lax.dot_general(dgp, wg, (((1,), (0,)), ((), ())), preferred_element_type=f32)
    part = part + lax.dot_general(dup, wu, (((1,), (0,)), ((), ())), preferred_element_type=f32)
    d_tokens = lax.psum_scatter(part.astype(jnp.bfloat16), AXES, scatter_dimension=0, tiled=True)
    d_gate = lax.dot_general(dgp, rows_x, tn, preferred_element_type=f32).astype(jnp.bfloat16)
    d_up = lax.dot_general(dup, rows_x, tn, preferred_element_type=f32).astype(jnp.bfloat16)
    d_down = lax.dot_general(hs, rows_g, tn, preferred_element_type=f32).astype(jnp.bfloat16)
    wide = lax.dynamic_update_slice(jnp.zeros((count, local * owners), f32), dprob, (0, first))
    mineprob = lax.psum_scatter(wide.astype(jnp.bfloat16), AXES, scatter_dimension=0, tiled=True)
    d_probs = jnp.sum(jnp.where(hit, mineprob.astype(f32)[:, None, :], 0.0), axis=2).astype(jnp.bfloat16)
    shape = (local, units, width)
    return (d_tokens, d_probs, d_gate.reshape(shape), d_up.reshape(shape), d_down.reshape(shape))


def solution(mesh):
    tok = P(AXES, None)
    wt = P("expert", "tensor", None)
    return jax.shard_map(
        per_device, mesh=mesh, in_specs=(tok, tok, tok, tok, wt, wt, wt),
        out_specs=(tok, tok, wt, wt, wt), check_vma=False
    )
```

time: 484 us -> 515 us (1.064); the launches traced: 475 us -> 515 us
  waiting for transfers between devices: 263 us -> 378 us
  local copies, waits for them, and re-layouts: 49.9 us -> 4.86 us
  matrix products: 60.5 us -> 50.2 us
  starting transfers between devices: 9.1 us -> 0.16 us
  blocking collectives: 73.1 us -> 64.8 us
    reduce_scatter x0 -> x2, waiting for transfers between devices: none -> 260 us  [the longest x1 132 us: per_device(): lax.psum_scatter(wide.astype(jnp.bfloat16), AXES, scatter_dimension=0, ti...]
    all_to_all x2 -> x0, waiting for transfers between devices: 115 us -> none  [the longest x1 115 us: per_device(): lax.all_to_all(block_terms, ('expert', 'tensor'), split_axis=0, concat_ax...]
    all_to_all x3 -> x0, blocking collectives: 57.2 us -> none  [the longest x1 26.1 us: per_device(): lax.all_to_all(send_x, 'expert', split_axis=0, concat_axis=0, tiled=True)]
    all_gather x1, blocking collectives: 15.9 us -> 64.8 us  [per_device(): probs = lax.all_gather(table, AXES, axis=0, tiled=True)]
    all_gather x2, waiting for transfers between devices: 148 us -> 117 us  [the longest x1 67.1 us: per_device(): rows_x = lax.all_gather(tokens, AXES, axis=0, tiled=True)]
    reshape x6 -> x1, local copies, waits for them, and re-layouts: 26.4 us -> 0.85 us  [per_device(): dprob = jnp.sum((hidden * back).reshape(count, local, units), axis=2)]
    all_gather x2 -> x0, local copies, waits for them, and re-layouts: 20.7 us -> none  [the longest x1 10.4 us: per_device(): lax.all_gather(moved[0], 'tensor', axis=1, tiled=True)]
    dot_general x13 -> x8, matrix products: 60.5 us -> 50.2 us  [the longest x1 9.49 us: per_device(): back = lax.dot_general(rows_g, wd, nt, preferred_element_type=f32)]
  transfers between devices with their start and end apart: 4 -> 4, of which waited for: 3 -> 4; matrix products, arithmetic and copies ran while one was open for 15% -> 6% of each run, Pallas kernels for 0% -> 0%
where the time goes in v1:
time: 515 us
  waiting for transfers between devices  378 us (73%)
  blocking collectives  64.8 us (13%)
  matrix products  50.2 us (10%)
  between operations  14 us (3%)
    reduce_scatter x1, waiting for transfers between devices, per_device(): lax.psum_scatter(wide.astype(jnp.bfloat16), AXES, scatter_dimension=0, ti...  132 us
    reduce_scatter x1, waiting for transfers between devices, per_device(): lax.psum_scatter(part.astype(jnp.bfloat16), AXES, scatter_dimension=0, ti...  127 us
    all_gather x1, waiting for transfers between devices, per_device(): rows_x = lax.all_gather(tokens, AXES, axis=0, tiled=True)  67.1 us
    all_gather x1, blocking collectives, per_device(): probs = lax.all_gather(table, AXES, axis=0, tiled=True)  64.8 us
    all_gather x1, waiting for transfers between devices, per_device(): rows_g = lax.all_gather(grad_out, AXES, axis=0, tiled=True)  50 us
  transfers between devices with their start and end apart: 4, of which 4 were waited for; matrix products, arithmetic and copies ran while one was open for 6% of the time, Pallas kernels for 0%

profile of v1, /device:TPU:0, one launch (start us, length us, event | category | flops | bytes accessed | tf_op | source)
XLA Modules:
  0.0 514.9 jit_solution(6247129796937112394)
XLA Ops:
  7.2 0.7 all-gather.5.cloned.1.call-update
  7.9 0.7 all-gather.3.cloned.1.call-update
  8.7 67.1 %all-gather.5.cloned.1.call-done = bf16[512,4096]{1,0:T(8,128)(2,1)} async-done(((bf16[16,4096]{1,0:T(8,128)(2,1)}), bf16[512,4096]{1,0:T(8,128)(2,1)}) %all-gather.5.cloned.1.call-update) | async-done | bytes 4194320 | tf_op jit(solution)/shard_map/all_gather | solution.py:18
  75.8 8.8 %fusion.3 = f32[512,768]{1,0:T(8,128)} fusion(bf16[512,4096]{1,0:T(8,128)(2,1)} %all-gather.5.cloned.1.call-done, bf16[768,4096]{1,0:T(8,128)(2,1)} %bitcast.33), kind=kOutput, calls=%fused_computation.15 | convolution fusion | flops 3221225472 | bytes 12058624 | tf_op jit(solution)/shard_map/dot_general | solution.py:30
  84.6 4.8 fusion.4
  89.5 50.0 %all-gather.3.cloned.1.call-done = bf16[512,4096]{1,0:T(8,128)(2,1)} async-done(((bf16[16,4096]{1,0:T(8,128)(2,1)}), bf16[512,4096]{1,0:T(8,128)(2,1)}) %all-gather.3.cloned.1.call-update) | async-done | bytes 4194320 | tf_op jit(solution)/shard_map/all_gather | solution.py:19
  139.5 9.5 %multiply_multiply_fusion = (f32[512,768]{1,0:T(8,128)S(1)}, f32[512,768]{1,0:T(8,128)}) fusion(f32[512,768]{1,0:T(8,128)} %fusion.3, f32[512,768]{1,0:T(8,128)} %fusion.4, bf16[512,4096]{1,0:T(8,128)(2,1)} %all-gather.3.cloned.1.call-done, bf16[768,4096]{1,0:T(8,128)(2,1)} %bitcast.32), kind=kOutput, calls=%fused_computation.10 | convolution fusion | flops 3223584768 | bytes 16777216 | tf_op jit(solution)/shard_map/dot_general | solution.py:31
  149.0 0.8 reshape.43
  149.8 0.7 reduce_sum.28
  151.0 0.6 copy-done.5
  151.9 132.3 %reduce-scatter.5.cloned.1.call-done = bf16[16,16]{1,0:T(8,128)(2,1)} async-done(((bf16[512,16]{1,0:T(8,128)(2,1)}), bf16[16,16]{1,0:T(8,128)(2,1)}) %reduce-scatter.5.cloned.1.call-update) | async-done | bytes 528 | tf_op jit(solution)/shard_map/reduce_scatter | solution.py:48
  284.2 0.8 convert_element_type.47
  285.2 64.8 %all_gather.9 = bf16[512,16]{1,0:T(8,128)(2,1)S(1)} all-gather(bf16[16,16]{1,0:T(8,128)(2,1)S(1)} %get-tuple-element.11), channel_id=1, replica_groups=mesh['expert'=8,'tensor'=4] {'expert','tensor'}, dimensions={0}, use_global_device_ids=true | all-gather | bytes 16896 | tf_op jit(solution)/shard_map/all_gather | solution.py:20
  350.1 0.6 broadcast_in_dim.37
  350.9 0.9 multiply_convert_fusion.1
  351.8 0.5 slice-done.2
  352.3 0.9 slice-done.3
  353.2 3.5 fusion.5
  356.7 5.1 add_convert_fusion
  361.7 0.7 copy.16
  362.4 7.7 %convolution_convert_fusion.2 = bf16[768,4096]{1,0:T(8,128)(2,1)} fusion(bf16[512,768]{1,0:T(8,128)(2,1)S(1)} %get-tuple-element.13, bf16[512,4096]{1,0:T(8,128)(2,1)} %all-gather.5.cloned.1.call-done), kind=kOutput, calls=%fused_computation.3 | convolution fusion | flops 3224371200 | bytes 11272192 | tf_op jit(solution)/shard_map/dot_general | solution.py:44
  370.1 5.4 %convolution_convert_fusion.1 = bf16[768,4096]{1,0:T(8,128)(2,1)} fusion(bf16[512,768]{1,0:T(8,128)(2,1)S(1)} %get-tuple-element.12, bf16[512,4096]{1,0:T(8,128)(2,1)S(1)} %copy-done.9), kind=kOutput, calls=%fused_computation.2 | convolution fusion | flops 3224371200 | bytes 11272192 | tf_op jit(solution)/shard_map/dot_general | solution.py:45
  375.5 5.6 %convolution_convert_fusion = bf16[768,4096]{1,0:T(8,128)(2,1)} fusion(bf16[512,4096]{1,0:T(8,128)(2,1)S(1)} %copy-done.10, f32[512,768]{1,0:T(8,128)S(1)} %bitcast.31, f32[512,768]{1,0:T(8,128)S(1)} %copy-done.1, f32[512,768]{1,0:T(8,128)S(1)} %copy-done.3), kind=kOutput, calls=%fused_computation.1 | convolution fusion | flops 3227123712 | bytes 15204352 | tf_op jit(solution)/shard_map/dot_general | solution.py:46
  381.1 127.3 %reduce-scatter.3.cloned.1.call-done = bf16[16,4096]{1,0:T(8,128)(2,1)} async-done(((bf16[512,4096]{1,0:T(8,128)(2,1)}), bf16[16,4096]{1,0:T(8,128)(2,1)}) %reduce-scatter.3.cloned.1.call-update) | async-done | bytes 131088 | tf_op jit(solution)/shard_map/reduce_scatter | solution.py:43
  (47 shorter events, 1.2 us)
Async XLA Ops:
  7.2 68.7 %all-gather.5.cloned.1.call-start = ((), (), s32[]{:S(2)}) async-start(), calls=%async_computation.3 | async-start | bytes 4325376 | tf_op jit(solution)/shard_map/all_gather | solution.py:18
  7.2 77.4 %slice-start = ((s8[6291456]{0:T(1024)(128)(4,1)}), s8[2097152]{0:T(1024)(128)(4,1)S(1)}, s32[]{:S(2)}) async-start(s8[6291456]{0:T(1024)(128)(4,1)} %bitcast.24), calls=%async_computation.6 | async-start | bytes 4194304
  7.9 131.6 %all-gather.3.cloned.1.call-start = ((), (), s32[]{:S(2)}) async-start(), calls=%async_computation.2 | async-start | bytes 4325376 | tf_op jit(solution)/shard_map/all_gather | solution.py:19
  8.6 275.5 %reduce-scatter.5.cloned.1.call-start = ((), (), s32[]{:S(2)}) async-start(), calls=%async_computation.5 | async-start | bytes 135168 | tf_op jit(solution)/shard_map/reduce_scatter | solution.py:48
  75.8 8.8 %slice-start.1 = ((s8[6291456]{0:T(1024)(128)(4,1)}), s8[4194304]{0:T(1024)(128)(4,1)S(1)}, s32[]{:S(2)}) async-start(s8[6291456]{0:T(1024)(128)(4,1)} %bitcast.24), calls=%async_computation.7 | async-start | bytes 8388608
  75.8 8.8 %copy-start.8 = (bf16[512,4096]{1,0:T(8,128)(2,1)S(1)}, bf16[512,4096]{1,0:T(8,128)(2,1)}, u32[]{:S(2)}) copy-start(bf16[512,4096]{1,0:T(8,128)(2,1)} %all-gather.5.cloned.1.call-done) | copy-start | bytes 12582916
  149.0 2.7 copy-start.6
  149.0 2.8 copy-start.7
  151.0 0.7 copy-start.5
  151.7 356.7 %reduce-scatter.3.cloned.1.call-start = ((), (), s32[]{:S(2)}) async-start(), calls=%async_computation.4 | async-start | bytes 4325376 | tf_op jit(solution)/shard_map/reduce_scatter | solution.py:43
  284.2 66.7 %copy-start = (f32[512,768]{1,0:T(8,128)S(1)}, f32[512,768]{1,0:T(8,128)}, u32[]{:S(2)}) copy-start(f32[512,768]{1,0:T(8,128)} %fusion.3) | copy-start | bytes 4718596
  284.2 66.7 %copy-start.2 = (f32[512,768]{1,0:T(8,128)S(1)}, f32[512,768]{1,0:T(8,128)}, u32[]{:S(2)}) copy-start(f32[512,768]{1,0:T(8,128)} %fusion.4) | copy-start | bytes 4718596
  284.2 66.7 %copy-start.4 = (f32[512,768]{1,0:T(8,128)S(1)}, f32[512,768]{1,0:T(8,128)}, u32[]{:S(2)}) copy-start(f32[512,768]{1,0:T(8,128)} %get-tuple-element.15) | copy-start | bytes 4718596
  350.1 2.2 slice-start.2
  350.9 2.3 slice-start.3
  350.9 5.8 %slice-start.4 = ((s8[6291456]{0:T(1024)(128)(4,1)}), s8[4194304]{0:T(1024)(128)(4,1)S(1)}, s32[]{:S(2)}) async-start(s8[6291456]{0:T(1024)(128)(4,1)} %bitcast.34), calls=%async_computation.10 | async-start | bytes 8388608
  353.2 3.5 slice-start.5
  362.4 7.7 %copy-start.9 = (bf16[512,4096]{1,0:T(8,128)(2,1)S(1)}, bf16[512,4096]{1,0:T(8,128)(2,1)}, u32[]{:S(2)}) copy-start(bf16[512,4096]{1,0:T(8,128)(2,1)} %all-gather.5.cloned.1.call-done) | copy-start | bytes 12582916
  370.1 5.4 %copy-start.1 = (f32[512,768]{1,0:T(8,128)S(1)}, f32[512,768]{1,0:T(8,128)}, u32[]{:S(2)}) copy-start(f32[512,768]{1,0:T(8,128)} %fusion.3) | copy-start | bytes 4718596
  370.1 5.4 %copy-start.3 = (f32[512,768]{1,0:T(8,128)S(1)}, f32[512,768]{1,0:T(8,128)}, u32[]{:S(2)}) copy-start(f32[512,768]{1,0:T(8,128)} %fusion.4) | copy-start | bytes 4718596
  370.1 5.4 %copy-start.10 = (bf16[512,4096]{1,0:T(8,128)(2,1)S(1)}, bf16[512,4096]{1,0:T(8,128)(2,1)}, u32[]{:S(2)}) copy-start(bf16[512,4096]{1,0:T(8,128)(2,1)} %all-gather.3.cloned.1.call-done) | copy-start | bytes 12582916
Sparse Core Ops, SparseCore 0:
  11.0 64.7 all-gather.4
  78.8 60.6 all-gather.2
  151.8 132.3 reduce-scatter.4
  361.9 146.4 reduce-scatter.2

commit v2 on v1

--- a/solution.py
+++ b/solution.py
@@ -1,9 +1,466 @@
 import jax
 import jax.numpy as jnp
 from jax import lax
+from jax.experimental import pallas as pl
+from jax.experimental.pallas import tpu as pltpu
 from jax.sharding import PartitionSpec as P
 
 AXES = ("expert", "tensor")
+CHUNK = 512
+LAG = 2
+NT = (((1,), (1,)), ((), ()))
+F32 = jnp.float32
+B16 = jnp.bfloat16
+
+
+def gather_and_send_back(tensor, tok, width, local, units):
+    chunks = width // CHUNK
+    half = CHUNK // 2
+    group = tensor * tok
+    hid = local * units
+    others = tensor - 1
+
+    def body(x_in, g_in, t_in, wg_in, wu_in, wd_in,
+             dx_out, dp_out, xs_out, gs_out, dg_out, du_out, hs_out,
+             xbuf, gbuf, tbuf, wgb, wub, wdb, gate, up, back, dgp, dup, hs,
+             pbuf, sbuf, ybuf, xb, azb, cxb, czb, cyb,
+             dpb, dps, dpy, dpx, dpz,
+             lsem, wsem, osem, hsem,
+             ax_s, ax_r, ag_s, ag_r, ss_s, ss_r, sa_s, sa_r, sc_s, sc_r):
+        e = lax.axis_index("expert")
+        z = lax.axis_index("tensor")
+        core = e % 2
+        bx = (e // 2) % 2
+        by = e // 4
+        to_s, to_x, to_y = 1 - 2 * core, 2 - 4 * bx, 4 - 8 * by
+        e_s, e_x, e_y, e_d = e + to_s, e + to_x, e + to_y, e + to_x + to_y
+        mine = (e, e_x, e_y, e_d)
+
+        def dev(expert, place):
+            return {"expert": expert, "tensor": place}
+
+        sib, xpeer, ypeer = dev(e_s, z), dev(e_x, z), dev(e_y, z)
+        zpeer = [None] + [dev(e, (z + k) % tensor) for k in range(1, tensor)]
+        zfrom = [None] + [(z + tensor - k) % tensor for k in range(1, tensor)]
+        zto = [None] + [(z + k) % tensor for k in range(1, tensor)]
+
+        def grp(expert):
+            return pl.ds(pl.multiple_of(expert * group, group), group)
+
+        def row(expert, place):
+            return pl.ds(pl.multiple_of((expert * tensor + place) * tok, tok), tok)
+
+        def rc(src, dst, s, r, to):
+            return pltpu.make_async_remote_copy(
+                src_ref=src, dst_ref=dst, send_sem=s, recv_sem=r, device_id=to,
+                device_id_type=pl.DeviceIdType.MESH)
+
+        own = row(e, z)
+        for c in range(chunks):
+            cols = pl.ds(c * CHUNK, CHUNK)
+            pltpu.make_async_copy(x_in.at[:, cols], xbuf.at[c, own], lsem.at[0, c]).start()
+            pltpu.make_async_copy(g_in.at[:, cols], gbuf.at[c, own], lsem.at[1, c]).start()
+        pltpu.make_async_copy(t_in, tbuf.at[0, own], lsem.at[0, chunks]).start()
+
+        barrier = pltpu.get_barrier_semaphore()
+        for to in [sib, xpeer, ypeer] + zpeer[1:]:
+            pl.semaphore_signal(barrier, inc=1, device_id=to, device_id_type=pl.DeviceIdType.MESH)
+        for c in range(chunks):
+            cols = pl.ds(c * CHUNK, CHUNK)
+            for n, (src, dst) in enumerate(((wg_in, wgb), (wu_in, wub), (wd_in, wdb))):
+                pltpu.make_async_copy(src.at[:, cols], dst.at[c], wsem.at[n, c]).start()
+        gate[...] = jnp.zeros_like(gate)
+        up[...] = jnp.zeros_like(up)
+        back[...] = jnp.zeros_like(back)
+        for c in range(chunks):
+            cols = pl.ds(c * CHUNK, CHUNK)
+            pltpu.make_async_copy(x_in.at[:, cols], xbuf.at[c, own], lsem.at[0, c]).wait()
+            pltpu.make_async_copy(g_in.at[:, cols], gbuf.at[c, own], lsem.at[1, c]).wait()
+        pltpu.make_async_copy(t_in, tbuf.at[0, own], lsem.at[0, chunks]).wait()
+        pl.semaphore_wait(barrier, 3 + others)
+
+        def a_z(buf, i, q, k, source=False):
+            rows = row(e, zfrom[k]) if source else own
+            return rc(buf.at[i, rows], buf.at[i, rows], ax_s.at[q, k - 1], ax_r.at[q, k - 1], zpeer[k])
+
+        def a_g(buf, i, q, n, expert, to):
+            rows = grp(expert)
+            return rc(buf.at[i, rows], buf.at[i, rows], ax_s.at[q, others + n], ax_r.at[q, others + n], to)
+
+        a_sends = ((0, e, xpeer), (1, e, ypeer), (2, e_x, ypeer), (3, e, sib), (4, e_x, sib), (5, e_y, sib), (6, e_d, sib))
+        a_recvs = ((0, e_x, xpeer), (1, e_y, ypeer), (2, e_d, ypeer),
+                   (3, e_s, sib), (4, e_s + to_x, sib), (5, e_s + to_y, sib), (6, e_s + to_x + to_y, sib))
+
+        def a_send(buf, i, q, n):
+            a_g(buf, i, q, *a_sends[n]).start()
+
+        def a_recv(buf, i, q, n):
+            a_g(buf, i, q, *a_recvs[n]).wait_recv()
+
+        def gather_a(s, buf, i, q):
+            if s == 0:
+                for k in range(1, tensor):
+                    a_z(buf, i, q, k).start()
+            if s == 1:
+                for k in range(1, tensor):
+                    a_z(buf, i, q, k, True).wait_recv()
+                for n in (0, 1, 3):
+                    a_send(buf, i, q, n)
+            if s == 2:
+                a_recv(buf, i, q, 0)
+                for n in (2, 4):
+                    a_send(buf, i, q, n)
+            if s == 3:
+                a_recv(buf, i, q, 1)
+                a_send(buf, i, q, 5)
+                a_recv(buf, i, q, 2)
+                a_send(buf, i, q, 6)
+            if s == 4:
+                for n in (3, 4, 5, 6):
+                    a_recv(buf, i, q, n)
+
+        def gather_a_drain(buf, i, q):
+            for k in range(1, tensor):
+                a_z(buf, i, q, k).wait_send()
+            for n in range(7):
+                a_g(buf, i, q, *a_sends[n]).wait_send()
+
+        def c_y(i, source=False):
+            rows = row(e_y, z) if source else own
+            return rc(gbuf.at[i, rows], gbuf.at[i, rows], ag_s.at[i, 0], ag_r.at[i, 0], ypeer)
+
+        def c_z(i, k, n, source=False):
+            rows = row((e, e_y)[n], zfrom[k] if source else z)
+            at = 1 + n * others + k - 1
+            return rc(gbuf.at[i, rows], gbuf.at[i, rows], ag_s.at[i, at], ag_r.at[i, at], zpeer[k])
+
+        c_base = 1 + 2 * others
+
+        def c_g(i, n, expert, to):
+            rows = grp(expert)
+            return rc(gbuf.at[i, rows], gbuf.at[i, rows], ag_s.at[i, c_base + n], ag_r.at[i, c_base + n], to)
+
+        c_sends = ((0, e, xpeer), (1, e_y, xpeer), (2, e, sib), (3, e_y, sib), (4, e_x, sib), (5, e_d, sib))
+        c_recvs = ((0, e_x, xpeer), (1, e_d, xpeer), (2, e_s, sib), (3, e_s + to_y, sib),
+                   (4, e_s + to_x, sib), (5, e_s + to_x + to_y, sib))
+
+        def gather_c(s, i):
+            if s == 0:
+                c_y(i).start()
+                for k in range(1, tensor):
+                    c_z(i, k, 0).start()
+            if s == 1:
+                c_y(i, True).wait_recv()
+                for k in range(1, tensor):
+                    c_z(i, k, 1).start()
+            if s == 2:
+                for k in range(1, tensor):
+                    c_z(i, k, 0, True).wait_recv()
+                for n in (0, 2):
+                    c_g(i, *c_sends[n]).start()
+                for k in range(1, tensor):
+                    c_z(i, k, 1, True).wait_recv()
+                for n in (1, 3):
+                    c_g(i, *c_sends[n]).start()
+            if s == 3:
+                for n in (0, 1):
+                    c_g(i, *c_recvs[n]).wait_recv()
+                    c_g(i, *c_sends[n + 4]).start()
+            if s == 4:
+                for n in (2, 3, 4, 5):
+                    c_g(i, *c_recvs[n]).wait_recv()
+
+        def gather_c_drain(i):
+            c_y(i).wait_send()
+            for k in range(1, tensor):
+                c_z(i, k, 0).wait_send()
+                c_z(i, k, 1).wait_send()
+            for n in range(6):
+                c_g(i, *c_sends[n]).wait_send()
+
+        def save_x(j):
+            at = pl.ds(pl.multiple_of(j * CHUNK, CHUNK), CHUNK)
+            return (pltpu.make_async_copy(xbuf.at[j], xs_out.at[:, at], osem.at[0, j]),
+                    pltpu.make_async_copy(gbuf.at[j], gs_out.at[:, at], osem.at[1, j]))
+
+        steps = chunks + 4 * LAG
+
+        def gather_step(t, carry):
+            for s in range(5):
+                j = t - s * LAG
+
+                @pl.when(t == s * LAG)
+                def _():
+                    gather_a(s, tbuf, 0, chunks)
+
+                @pl.when(jnp.logical_and(j >= 0, j < chunks))
+                def _():
+                    gather_a(s, xbuf, j, j)
+                    gather_c(s, j)
+                    if s == 4:
+                        for c in save_x(j):
+                            c.start()
+                        for n, (src, dst) in enumerate(((wg_in, wgb), (wu_in, wub), (wd_in, wdb))):
+                            pltpu.make_async_copy(src.at[:, pl.ds(0, CHUNK)], dst.at[j], wsem.at[n, j]).wait()
+                        gate[...] += lax.dot_general(xbuf[j], wgb[j], NT, preferred_element_type=F32)
+                        up[...] += lax.dot_general(xbuf[j], wub[j], NT, preferred_element_type=F32)
+                        back[...] += lax.dot_general(gbuf[j], wdb[j], NT, preferred_element_type=F32)
+            return carry
+
+        lax.fori_loop(0, steps, gather_step, 0)
+
+        block = 32
+        lane = lax.broadcasted_iota(jnp.int32, (block, tbuf.shape[2]), 1)
+
+        def hidden_step(b, carry):
+            rows = pl.ds(pl.multiple_of(b * block, block), block)
+            table = tbuf[0, rows, :].astype(F32)
+            placed = jnp.zeros((block, tbuf.shape[2]), F32)
+            for n in range(local):
+                cols = pl.ds(n * units, units)
+                here = lane == e * local + n
+                p = jnp.sum(jnp.where(here, table, 0.0), axis=1, keepdims=True)
+                gv, uv, bv = gate[rows, cols], up[rows, cols], back[rows, cols]
+                sg = jax.nn.sigmoid(gv)
+                act = gv * sg
+                hv = act * uv
+                pb = p * bv
+                dgp[rows, cols] = (pb * uv * sg * (1.0 + gv * (1.0 - sg))).astype(B16)
+                dup[rows, cols] = (pb * act).astype(B16)
+                hs[rows, cols] = (hv * p).astype(B16)
+                placed = placed + jnp.where(here, jnp.sum(hv * bv, axis=1, keepdims=True), 0.0)
+            dpb[0, rows, :] = placed.astype(B16)
+            return carry
+
+        lax.fori_loop(0, gate.shape[0] // block, hidden_step, 0)
+        saves = [pltpu.make_async_copy(a, b, hsem.at[n])
+                 for n, (a, b) in enumerate(((dgp, dg_out), (dup, du_out), (hs, hs_out)))]
+        for c in saves:
+            c.start()
+
+        order = (3, 2, 1, 0)
+
+        def slot(n):
+            return pl.ds(n * group, group)
+
+        def back_s(p, d, i, q, n):
+            return rc(p.at[i, grp(mine[n] + to_s)], d.at[i, slot(n)], ss_s.at[q, n], ss_r.at[q, n], sib)
+
+        def merge_s(p, d, i, q):
+            for n in order:
+                back_s(p, d, i, q, n).wait_recv()
+                p[i, grp(mine[n]), :] = (p[i, grp(mine[n]), :].astype(F32)
+                                         + d[i, slot(n), :].astype(F32)).astype(B16)
+
+        def add(p, i, rows, cols, term):
+            p[i, rows, cols] = (p[i, rows, cols].astype(F32) + term).astype(B16)
+
+        def a_back(p, y_, x_, z_, i, q, cols, kind, n):
+            if kind == 0:
+                return rc(p.at[i, grp((e_y, e_d)[n]), cols], y_.at[i, slot(n)], sa_s.at[q, n], sa_r.at[q, n], ypeer)
+            if kind == 1:
+                return rc(p.at[i, grp(e_x), cols], x_.at[i], sa_s.at[q, 2], sa_r.at[q, 2], xpeer)
+            return rc(p.at[i, row(e, zto[n]), cols], z_.at[i, pl.ds((n - 1) * tok, tok)],
+                      sa_s.at[q, 2 + n], sa_r.at[q, 2 + n], zpeer[n])
+
+        def scatter_a(s, bufs, i, q, cols, out, at):
+            p, y_, x_, z_ = bufs
+            args = (p, y_, x_, z_, i, q, cols)
+            if s == 1:
+                for n in (1, 0):
+                    a_back(*args, 0, n).start()
+            if s == 2:
+                for n in (1, 0):
+                    a_back(*args, 0, n).wait_recv()
+                    add(p, i, grp((e, e_x)[n]), cols, y_[i, slot(n), :].astype(F32))
+                    if n == 1:
+                        a_back(*args, 1, 0).start()
+            if s == 3:
+                a_back(*args, 1, 0).wait_recv()
+                add(p, i, grp(e), cols, x_[i].astype(F32))
+                for k in range(1, tensor):
+                    a_back(*args, 2, k).start()
+            if s == 4:
+                total = p[i, own, cols].astype(F32)
+                for k in range(1, tensor):
+                    a_back(*args, 2, k).wait_recv()
+                    total = total + z_[i, pl.ds((k - 1) * tok, tok), :].astype(F32)
+                out[:, at] = total.astype(B16)
+
+        def scatter_a_drain(bufs, i, q, cols):
+            args = (*bufs, i, q, cols)
+            for n in (0, 1):
+                a_back(*args, 0, n).wait_send()
+            a_back(*args, 1, 0).wait_send()
+            for k in range(1, tensor):
+                a_back(*args, 2, k).wait_send()
+
+        ccols = pl.ds(half, half)
+
+        def c_back(i, kind, n, m=0):
+            if kind == 0:
+                return rc(pbuf.at[i, grp((e_x, e_d)[n]), ccols], cxb.at[i, slot(n)], sc_s.at[i, n], sc_r.at[i, n], xpeer)
+            if kind == 1:
+                at = m * others + n - 1
+                return rc(pbuf.at[i, row((e, e_y)[m], zto[n]), ccols], czb.at[i, pl.ds(at * tok, tok)],
+                          sc_s.at[i, 2 + at], sc_r.at[i, 2 + at], zpeer[n])
+            at = 2 + 2 * others
+            return rc(pbuf.at[i, row(e_y, z), ccols], cyb.at[i], sc_s.at[i, at], sc_r.at[i, at], ypeer)
+
+        def scatter_c(s, i, out, at):
+            if s == 1:
+                for n in (1, 0):
+                    c_back(i, 0, n).start()
+            if s == 2:
+                for n in (1, 0):
+                    c_back(i, 0, n).wait_recv()
+                    add(pbuf, i, grp((e, e_y)[n]), ccols, cxb[i, slot(n), :].astype(F32))
+                    for k in range(1, tensor):
+                        c_back(i, 1, k, n).start()
+            if s == 3:
+                for m in (1, 0):
+                    total = jnp.zeros((tok, half), F32)
+                    for k in range(1, tensor):
+                        c_back(i, 1, k, m).wait_recv()
+                        total = total + czb[i, pl.ds((m * others + k - 1) * tok, tok), :].astype(F32)
+                    add(pbuf, i, row((e, e_y)[m], z), ccols, total)
+                    if m == 1:
+                        c_back(i, 2, 0).start()
+            if s == 4:
+                c_back(i, 2, 0).wait_recv()
+                out[:, at] = (pbuf[i, own, ccols].astype(F32) + cyb[i].astype(F32)).astype(B16)
+
+        def scatter_c_drain(i):
+            for n in (0, 1):
+                c_back(i, 0, n).wait_send()
+            for m in (0, 1):
+                for k in range(1, tensor):
+                    c_back(i, 1, k, m).wait_send()
+            c_back(i, 2, 0).wait_send()
+
+        acols = pl.ds(0, half)
+        big = (pbuf, ybuf, xb, azb)
+        small = (dpb, dpy, dpx, dpz)
+        all_cols = pl.ds(0, tbuf.shape[2])
+
+        def scatter_step(t, carry):
+            @pl.when(t < chunks)
+            def _():
+                part = jnp.dot(dgp[...], wgb[t], preferred_element_type=F32)
+                part = part + jnp.dot(dup[...], wub[t], preferred_element_type=F32)
+                pbuf[t] = part.astype(B16)
+
+            for s in range(5):
+                j = t - s * LAG
+
+                @pl.when(t == s * LAG)
+                def _():
+                    if s == 0:
+                        for n in order:
+                            back_s(dpb, dps, 0, chunks, n).start()
+                    if s == 1:
+                        merge_s(dpb, dps, 0, chunks)
+                    scatter_a(s, small, 0, chunks, all_cols, dp_out, all_cols)
+
+                @pl.when(jnp.logical_and(j >= 0, j < chunks))
+                def _():
+                    if s == 0:
+                        for n in order:
+                            back_s(pbuf, sbuf, j, j, n).start()
+                    if s == 1:
+                        merge_s(pbuf, sbuf, j, j)
+                    a_at = pl.ds(pl.multiple_of(j * CHUNK, CHUNK), half)
+                    c_at = pl.ds(pl.multiple_of(j * CHUNK + half, half), half)
+                    scatter_a(s, big, j, j, acols, dx_out, a_at)
+                    scatter_c(s, j, dx_out, c_at)
+            return carry
+
+        lax.fori_loop(0, steps, scatter_step, 0)
+
+        gather_a_drain(tbuf, 0, chunks)
+        for n in order:
+            back_s(dpb, dps, 0, chunks, n).wait_send()
+        scatter_a_drain(small, 0, chunks, all_cols)
+
+        def drain(j, carry):
+            gather_a_drain(xbuf, j, j)
+            gather_c_drain(j)
+            for n in order:
+                back_s(pbuf, sbuf, j, j, n).wait_send()
+            scatter_a_drain(big, j, j, acols)
+            scatter_c_drain(j)
+            for c in save_x(j):
+                c.wait()
+            return carry
+
+        lax.fori_loop(0, chunks, drain, 0)
+        for c in saves:
+            c.wait()
+
+    return body
+
+
+def fused(tokens, grad_out, table, wg, wu, wd, tensor, local, units):
+    tok, width = tokens.shape
+    lanes = table.shape[1]
+    owners = lax.axis_size("expert")
+    rows = owners * tensor * tok
+    hid = local * units
+    chunks = width // CHUNK
+    half = CHUNK // 2
+    mid = owners // 2 * tensor * tok
+    two, one = 2 * tensor * tok, tensor * tok
+    oth = tensor - 1
+    V = pltpu.VMEM
+    dma = pltpu.SemaphoreType.DMA
+    scratch = [
+        V((chunks, rows, CHUNK), B16), V((chunks, rows, CHUNK), B16), V((1, rows, lanes), B16),
+        V((chunks, hid, CHUNK), B16), V((chunks, hid, CHUNK), B16), V((chunks, hid, CHUNK), B16),
+        V((rows, hid), F32), V((rows, hid), F32), V((rows, hid), F32),
+        V((rows, hid), B16), V((rows, hid), B16), V((rows, hid), B16),
+        V((chunks, rows, CHUNK), B16), V((chunks, mid, CHUNK), B16),
+        V((chunks, two, half), B16), V((chunks, one, half), B16), V((chunks, oth * tok, half), B16),
+        V((chunks, two, half), B16), V((chunks, 2 * oth * tok, half), B16), V((chunks, tok, half), B16),
+        V((1, rows, lanes), B16), V((1, mid, lanes), B16), V((1, two, lanes), B16), V((1, one, lanes), B16),
+        V((1, oth * tok, lanes), B16),
+        dma((2, chunks + 1)), dma((3, chunks)), dma((2, chunks)), dma((3,)),
+        dma((chunks + 1, oth + 7)), dma((chunks + 1, oth + 7)),
+        dma((chunks, 2 * oth + 7)), dma((chunks, 2 * oth + 7)),
+        dma((chunks + 1, 4)), dma((chunks + 1, 4)),
+        dma((chunks + 1, 3 + oth)), dma((chunks + 1, 3 + oth)),
+        dma((chunks, 3 + 2 * oth)), dma((chunks, 3 + 2 * oth)),
+    ]
+    any_, vm = pl.BlockSpec(memory_space=pl.ANY), pl.BlockSpec(memory_space=pltpu.VMEM)
+    sd = jax.ShapeDtypeStruct
+    return pl.pallas_call(
+        gather_and_send_back(tensor, tok, width, local, units),
+        out_shape=(sd((tok, width), B16), sd((tok, lanes), B16), sd((rows, width), B16), sd((rows, width), B16),
+                   sd((rows, hid), B16), sd((rows, hid), B16), sd((rows, hid), B16)),
+        in_specs=[any_] * 6,
+        out_specs=(vm, vm) + (any_,) * 5,
+        scratch_shapes=scratch,
+        compiler_params=pltpu.CompilerParams(collective_id=0, has_side_effects=True, vmem_limit_bytes=60 * 1024 * 1024),
+        cost_estimate=pl.CostEstimate(flops=10 * rows * hid * width, transcendentals=rows * hid,
+                                      bytes_accessed=6 * hid * width + 8 * rows * width),
+        name="gather_and_send_back",
+    )(tokens, grad_out, table, wg, wu, wd)
+
+
+def with_kernel(tokens, grad_out, routes, gate_probs, w_gate, w_up, w_down):
+    local, units, width = w_gate.shape
+    tensor = lax.axis_size("tensor")
+    ids = jnp.arange(128, dtype=jnp.int32)
+    hit = routes[:, :, None] == ids[None, None, :]
+    table = jnp.sum(jnp.where(hit, gate_probs[:, :, None].astype(F32), 0.0), axis=1).astype(B16)
+    flat = [w.reshape(local * units, width) for w in (w_gate, w_up, w_down)]
+    d_tokens, dp, xs, gs, dgp, dup, hs = fused(tokens, grad_out, table, *flat, tensor, local, units)
+    tn = (((0,), (0,)), ((), ()))
+    shape = (local, units, width)
+    d_gate = lax.dot_general(dgp, xs, tn, preferred_element_type=F32).astype(B16).reshape(shape)
+    d_up = lax.dot_general(dup, xs, tn, preferred_element_type=F32).astype(B16).reshape(shape)
+    d_down = lax.dot_general(hs, gs, tn, preferred_element_type=F32).astype(B16).reshape(shape)
+    d_probs = jnp.sum(jnp.where(hit, dp.astype(F32)[:, None, :], 0.0), axis=2).astype(B16)
+    return (d_tokens, d_probs, d_gate, d_up, d_down)
 
 
 def per_device(tokens, grad_out, routes, gate_probs, w_gate, w_up, w_down):
@@ -54,7 +511,15 @@
 def solution(mesh):
     tok = P(AXES, None)
     wt = P("expert", "tensor", None)
-    return jax.shard_map(
-        per_device, mesh=mesh, in_specs=(tok, tok, tok, tok, wt, wt, wt),
-        out_specs=(tok, tok, wt, wt, wt), check_vma=False
-    )
+
+    def program(tokens, grad_out, routes, gate_probs, w_gate, w_up, w_down):
+        small = tokens.shape[0] <= 512 and mesh.shape["expert"] == 8 and mesh.shape["tensor"] > 1
+        small = small and tokens.shape[0] // mesh.size == 16 and tokens.shape[1] % CHUNK == 0
+        small = small and w_gate.shape[0] <= 128 and w_gate.shape[0] == 16
+        small = small and w_gate.shape[1] // mesh.shape["tensor"] <= 384 and w_gate.shape[2] <= 4096
+        return jax.shard_map(
+            with_kernel if small else per_device, mesh=mesh, in_specs=(tok, tok, tok, tok, wt, wt, wt),
+            out_specs=(tok, tok, wt, wt, wt), check_vma=False
+        )(tokens, grad_out, routes, gate_probs, w_gate, w_up, w_down)
+
+    return program

time: 515 us -> 120 us (0.23)
  waiting for transfers between devices: 378 us -> 0 us
  Pallas kernels: 0 us -> 94.9 us
  blocking collectives: 64.8 us -> 0 us
  matrix products: 50.2 us -> 19.4 us
  between operations: 14 us -> 0.66 us
    reduce_scatter x2 -> x0, waiting for transfers between devices: 260 us -> none  [the longest x1 132 us: per_device(): lax.psum_scatter(wide.astype(jnp.bfloat16), AXES, scatter_dimension=0, ti...]
    all_gather x2 -> x0, waiting for transfers between devices: 117 us -> none  [the longest x1 67.1 us: per_device(): rows_x = lax.all_gather(tokens, AXES, axis=0, tiled=True)]
    pallas_call x0 -> x1, Pallas kernels: none -> 94.9 us  [fused(): pl.pallas_call(gather_and_send_back(tensor, tok, width, local, units), ou...]
    all_gather x1 -> x0, blocking collectives: 64.8 us -> none  [per_device(): probs = lax.all_gather(table, AXES, axis=0, tiled=True)]
    dot_general x8 -> x3, matrix products: 50.2 us -> 19.4 us  [the longest x1 8.74 us: with_kernel(): lax.dot_general(dgp, xs, tn, preferred_element_type=F32).astype(B16)]
  transfers between devices with their start and end apart: 4 -> 0, of which waited for: 4 -> 0; matrix products, arithmetic and copies ran while one was open for 6% -> 0% of each run, Pallas kernels for 0% -> 0%
where the time goes in v2:
time: 120 us; the launch traced here: 119 us
  Pallas kernels  94.9 us (79%)
  matrix products  19.4 us (16%)
  local copies, waits for them, and re-layouts  2.85 us (2%)
  other arithmetic  1.56 us (1%)
    pallas_call x1, Pallas kernels, fused(): pl.pallas_call(gather_and_send_back(tensor, tok, width, local, units), ou...  94.9 us
    dot_general x1, matrix products, with_kernel(): lax.dot_general(dgp, xs, tn, preferred_element_type=F32).astype(B16)  8.74 us
    dot_general x1, matrix products, with_kernel(): lax.dot_general(dup, xs, tn, preferred_element_type=F32).astype(B16)  5.35 us
    dot_general x1, matrix products, with_kernel(): lax.dot_general(hs, gs, tn, preferred_element_type=F32).astype(B16)  5.35 us

profile of v2, /device:TPU:0, one launch (start us, length us, event | category | flops | bytes accessed | tf_op | source)
XLA Modules:
  0.0 119.5 jit_solution(1867247009465686685)
XLA Ops:
  0.6 0.8 copy.14
  1.4 0.8 copy.15
  2.1 0.7 select_reduce_fusion.1.t_in
  2.9 94.9 %gather_and_send_back.1 = (bf16[16,4096]{1,0:T(8,128)(2,1)}, bf16[16,128]{1,0:T(8,128)(2,1)}, bf16[512,4096]{1,0:T(8,128)(2,1)}, bf16[512,4096]{1,0:T(8,128)(2,1...) custom-call(bf16[16,4096]{1,0:T(8,128)(2,1)} %x_in.1, bf16[16,4096]{1,0:T(8,128)(2,1)} %g_in.1, ...), custom_call_target="tpu_custom_call" | custom-call | flops 16106127360 | bytes 35651584 | tf_op jit(solution)/shard_map/gather_and_send_back/pallas_call | solution.py:435
  97.8 0.7 convert_element_type.24
  98.5 0.2 select_reduce_fusion
  98.7 0.7 copy.16
  99.3 0.0 copy-start.2
  99.3 0.0 copy-start.4
  99.3 8.7 %convolution_convert_fusion.2 = bf16[768,4096]{1,0:T(8,128)(2,1)} fusion(bf16[512,768]{1,0:T(8,128)(2,1)} %get-tuple-element.14, bf16[512,4096]{1,0:T(8,128)(2,1)} %get-tuple-element.15), kind=kOutput, calls=%fused_computation.2 | convolution fusion | flops 3224371200 | bytes 11272192 | tf_op jit(solution)/shard_map/dot_general | solution.py:459
  108.1 0.0 copy-done.2
  108.1 0.0 copy-done.4
  108.1 0.0 copy-start.1
  108.1 0.0 copy-start.3
  108.1 5.4 %convolution_convert_fusion.1 = bf16[768,4096]{1,0:T(8,128)(2,1)} fusion(bf16[512,768]{1,0:T(8,128)(2,1)S(1)} %copy-done.4, bf16[512,4096]{1,0:T(8,128)(2,1)S(1)} %copy-done.2), kind=kOutput, calls=%fused_computation.1 | convolution fusion | flops 3224371200 | bytes 11272192 | tf_op jit(solution)/shard_map/dot_general | solution.py:460
  113.4 0.0 copy-done.1
  113.4 0.0 copy-done.3
  113.5 0.0 copy-start
  113.5 5.3 %convolution_convert_fusion = bf16[768,4096]{1,0:T(8,128)(2,1)} fusion(bf16[512,768]{1,0:T(8,128)(2,1)S(1)} %copy-done.3, bf16[512,4096]{1,0:T(8,128)(2,1)S(1)} %copy-done.1), kind=kOutput, calls=%fused_computation | convolution fusion | flops 3224371200 | bytes 11272192 | tf_op jit(solution)/shard_map/dot_general | solution.py:461
  118.8 0.0 copy-done
  118.8 0.7 copy.18
Async XLA Ops:
  99.3 8.8 %copy-start.2 = (bf16[512,4096]{1,0:T(8,128)(2,1)S(1)}, bf16[512,4096]{1,0:T(8,128)(2,1)}, u32[]{:S(2)}) copy-start(bf16[512,4096]{1,0:T(8,128)(2,1)} %get-tuple-element.15) | copy-start | bytes 12582916
  99.3 8.8 %copy-start.4 = (bf16[512,768]{1,0:T(8,128)(2,1)S(1)}, bf16[512,768]{1,0:T(8,128)(2,1)}, u32[]{:S(2)}) copy-start(bf16[512,768]{1,0:T(8,128)(2,1)} %get-tuple-element.16) | copy-start | bytes 2359300
  108.1 5.4 %copy-start.1 = (bf16[512,4096]{1,0:T(8,128)(2,1)S(1)}, bf16[512,4096]{1,0:T(8,128)(2,1)}, u32[]{:S(2)}) copy-start(bf16[512,4096]{1,0:T(8,128)(2,1)} %get-tuple-element.18) | copy-start | bytes 12582916
  108.1 5.4 %copy-start.3 = (bf16[512,768]{1,0:T(8,128)(2,1)S(1)}, bf16[512,768]{1,0:T(8,128)(2,1)}, u32[]{:S(2)}) copy-start(bf16[512,768]{1,0:T(8,128)(2,1)} %get-tuple-element.17) | copy-start | bytes 2359300
  113.5 5.4 %copy-start = (bf16[16,4096]{1,0:T(8,128)(2,1)S(1)}, bf16[16,4096]{1,0:T(8,128)(2,1)}, u32[]{:S(2)}) copy-start(bf16[16,4096]{1,0:T(8,128)(2,1)} %get-tuple-element.29) | copy-start | bytes 393220

commit v3 on v2

--- a/solution.py
+++ b/solution.py
@@ -196,7 +196,15 @@
                 @pl.when(jnp.logical_and(j >= 0, j < chunks))
                 def _():
                     gather_a(s, xbuf, j, j)
-                    gather_c(s, j)
+
+                    @pl.when(j % 4 != 3)
+                    def _():
+                        gather_c(s, j)
+
+                    @pl.when(j % 4 == 3)
+                    def _():
+                        gather_a(s, gbuf, j, chunks + 1 + j // 4)
+
                     if s == 4:
                         for c in save_x(j):
                             c.start()
@@ -384,7 +392,15 @@
 
         def drain(j, carry):
             gather_a_drain(xbuf, j, j)
-            gather_c_drain(j)
+
+            @pl.when(j % 4 != 3)
+            def _():
+                gather_c_drain(j)
+
+            @pl.when(j % 4 == 3)
+            def _():
+                gather_a_drain(gbuf, j, chunks + 1 + j // 4)
+
             for n in order:
                 back_s(pbuf, sbuf, j, j, n).wait_send()
             scatter_a_drain(big, j, j, acols)
@@ -424,7 +440,7 @@
         V((1, rows, lanes), B16), V((1, mid, lanes), B16), V((1, two, lanes), B16), V((1, one, lanes), B16),
         V((1, oth * tok, lanes), B16),
         dma((2, chunks + 1)), dma((3, chunks)), dma((2, chunks)), dma((3,)),
-        dma((chunks + 1, oth + 7)), dma((chunks + 1, oth + 7)),
+        dma((chunks + 1 + chunks // 4, oth + 7)), dma((chunks + 1 + chunks // 4, oth + 7)),
         dma((chunks, 2 * oth + 7)), dma((chunks, 2 * oth + 7)),
         dma((chunks + 1, 4)), dma((chunks + 1, 4)),
         dma((chunks + 1, 3 + oth)), dma((chunks + 1, 3 + oth)),

time: 120 us -> 118 us (0.983)
  Pallas kernels: 94.9 us -> 92.9 us
    pallas_call x1, Pallas kernels: 94.9 us -> 92.9 us  [fused(): pl.pallas_call(gather_and_send_back(tensor, tok, width, local, units), ou...]
where the time goes in v3:
time: 118 us; the launch traced here: 117 us
  Pallas kernels  92.9 us (79%)
  matrix products  19.4 us (16%)
  local copies, waits for them, and re-layouts  2.85 us (2%)
  other arithmetic  1.56 us (1%)
    pallas_call x1, Pallas kernels, fused(): pl.pallas_call(gather_and_send_back(tensor, tok, width, local, units), ou...  92.9 us
    dot_general x1, matrix products, with_kernel(): lax.dot_general(dgp, xs, tn, preferred_element_type=F32).astype(B16)  8.75 us
    dot_general x1, matrix products, with_kernel(): lax.dot_general(dup, xs, tn, preferred_element_type=F32).astype(B16)  5.35 us
    dot_general x1, matrix products, with_kernel(): lax.dot_general(hs, gs, tn, preferred_element_type=F32).astype(B16)  5.35 us

profile of v3, /device:TPU:0, one launch (start us, length us, event | category | flops | bytes accessed | tf_op | source)
XLA Modules:
  0.0 117.4 jit_solution(13915964909530346569)
XLA Ops:
  0.6 0.8 copy.14
  1.4 0.8 copy.15
  2.1 0.7 select_reduce_fusion.1.t_in
  2.9 92.9 %gather_and_send_back.1 = (bf16[16,4096]{1,0:T(8,128)(2,1)}, bf16[16,128]{1,0:T(8,128)(2,1)}, bf16[512,4096]{1,0:T(8,128)(2,1)}, bf16[512,4096]{1,0:T(8,128)(2,1...) custom-call(bf16[16,4096]{1,0:T(8,128)(2,1)} %x_in.1, bf16[16,4096]{1,0:T(8,128)(2,1)} %g_in.1, ...), custom_call_target="tpu_custom_call" | custom-call | flops 16106127360 | bytes 35651584 | tf_op jit(solution)/shard_map/gather_and_send_back/pallas_call | solution.py:451
  95.7 0.7 convert_element_type.24
  96.4 0.2 select_reduce_fusion
  96.6 0.7 copy.16
  97.3 0.0 copy-start.2
  97.3 0.0 copy-start.4
  97.3 8.7 %convolution_convert_fusion.2 = bf16[768,4096]{1,0:T(8,128)(2,1)} fusion(bf16[512,768]{1,0:T(8,128)(2,1)} %get-tuple-element.14, bf16[512,4096]{1,0:T(8,128)(2,1)} %get-tuple-element.15), kind=kOutput, calls=%fused_computation.2 | convolution fusion | flops 3224371200 | bytes 11272192 | tf_op jit(solution)/shard_map/dot_general | solution.py:475
  106.0 0.0 copy-done.2
  106.0 0.0 copy-done.4
  106.0 0.0 copy-start.1
  106.0 0.0 copy-start.3
  106.0 5.4 %convolution_convert_fusion.1 = bf16[768,4096]{1,0:T(8,128)(2,1)} fusion(bf16[512,768]{1,0:T(8,128)(2,1)S(1)} %copy-done.4, bf16[512,4096]{1,0:T(8,128)(2,1)S(1)} %copy-done.2), kind=kOutput, calls=%fused_computation.1 | convolution fusion | flops 3224371200 | bytes 11272192 | tf_op jit(solution)/shard_map/dot_general | solution.py:476
  111.4 0.0 copy-done.1
  111.4 0.0 copy-done.3
  111.4 0.0 copy-start
  111.4 5.3 %convolution_convert_fusion = bf16[768,4096]{1,0:T(8,128)(2,1)} fusion(bf16[512,768]{1,0:T(8,128)(2,1)S(1)} %copy-done.3, bf16[512,4096]{1,0:T(8,128)(2,1)S(1)} %copy-done.1), kind=kOutput, calls=%fused_computation | convolution fusion | flops 3224371200 | bytes 11272192 | tf_op jit(solution)/shard_map/dot_general | solution.py:477
  116.7 0.0 copy-done
  116.7 0.7 copy.18
Async XLA Ops:
  97.3 8.8 %copy-start.2 = (bf16[512,4096]{1,0:T(8,128)(2,1)S(1)}, bf16[512,4096]{1,0:T(8,128)(2,1)}, u32[]{:S(2)}) copy-start(bf16[512,4096]{1,0:T(8,128)(2,1)} %get-tuple-element.15) | copy-start | bytes 12582916
  97.3 8.8 %copy-start.4 = (bf16[512,768]{1,0:T(8,128)(2,1)S(1)}, bf16[512,768]{1,0:T(8,128)(2,1)}, u32[]{:S(2)}) copy-start(bf16[512,768]{1,0:T(8,128)(2,1)} %get-tuple-element.16) | copy-start | bytes 2359300
  106.0 5.4 %copy-start.1 = (bf16[512,4096]{1,0:T(8,128)(2,1)S(1)}, bf16[512,4096]{1,0:T(8,128)(2,1)}, u32[]{:S(2)}) copy-start(bf16[512,4096]{1,0:T(8,128)(2,1)} %get-tuple-element.18) | copy-start | bytes 12582916
  106.0 5.4 %copy-start.3 = (bf16[512,768]{1,0:T(8,128)(2,1)S(1)}, bf16[512,768]{1,0:T(8,128)(2,1)}, u32[]{:S(2)}) copy-start(bf16[512,768]{1,0:T(8,128)(2,1)} %get-tuple-element.17) | copy-start | bytes 2359300
  111.4 5.4 %copy-start = (bf16[16,4096]{1,0:T(8,128)(2,1)S(1)}, bf16[16,4096]{1,0:T(8,128)(2,1)}, u32[]{:S(2)}) copy-start(bf16[16,4096]{1,0:T(8,128)(2,1)} %get-tuple-element.29) | copy-start | bytes 393220
